TPU v7x, 256 devices: a whole 4x4x8 slice. The times are simulated.
256 devices in a mesh: px: 16 (over y, x), py: 16 (over z, core).
Axes of the slice: x: 4, y: 4, z: 8, core: 2. Of those that a mesh axis runs over, the one named last changes fastest.
Arguments:
- start_field: float32 [128, 256, 512], P('px', 'py'), may hold values from -1.7 to 1.7
- known: float32 [8, 128, 256, 512], P(None, 'px', 'py'), may hold values from -1 to 1
Outputs:
- solution_field: float32 [128, 256, 512], P('px', 'py')
- residual: float32 [128, 256, 512], P('px', 'py')
All inputs are finite; a program needn't handle non-finite values.
Results may differ from a plain program's by a relative error of at most 0.01.
Values sent between devices are 32-bit elements; how exact they have to be, the bound alone decides.
No kernel may reach another device: no remote copies, remote signals or barrier semaphores. Data moves between devices by JAX's collectives and lax.ppermute only.
A program may use at most 64 MiB of HBM per device.

v0:
```python
import jax
import jax.numpy as jnp
from jax import lax
from jax.sharding import PartitionSpec as P

NEWTON = 2
ITERS = 3
DIFFUSION = 0.5
SHIFT = 4.0
EPS = 1e-06


def extended(cells, sides, width):
    for axis, dim in sides:
        count = lax.axis_size(axis)
        ends = count - 1
        head = lax.slice_in_dim(cells, 0, width, axis=dim)
        tail = lax.slice_in_dim(cells, cells.shape[dim] - width, cells.shape[dim], axis=dim)
        cells = jnp.concatenate(
            [
                lax.ppermute(tail, axis, [(i, (i + 1) % count) for i in range(ends)]),
                cells,
                lax.ppermute(head, axis, [((i + 1) % count, i) for i in range(ends)]),
            ],
            axis=dim,
        )
    return cells


def laplace(field):
    padded = extended(field, (("px", 0), ("py", 1)), 1)
    zero = jnp.zeros_like(field[:, :, :1])
    upper = jnp.concatenate([field[:, :, 1:], zero], axis=2)
    lower = jnp.concatenate([zero, field[:, :, :-1]], axis=2)
    beside = padded[2:, 1:-1, :] + padded[:-2, 1:-1, :]
    beside = beside + padded[1:-1, 2:, :] + padded[1:-1, :-2, :]
    return beside + upper + lower - 6.0 * field


def allen_cahn(field, lap):
    return DIFFUSION * lap + field - field * field * field


def solve_small(hess, beta):
    normal = jnp.sum(hess[:, :, None] * hess[:, None, :], axis=0)
    target = beta * hess[0]
    lower = jnp.linalg.cholesky(normal)
    count = normal.shape[0]
    forward = []
    for i in range(count):
        acc = target[i]
        for j in range(i):
            acc = acc - lower[i, j] * forward[j]
        forward.append(acc / lower[i, i])
    back = [None] * count
    for i in reversed(range(count)):
        acc = forward[i]
        for j in range(i + 1, count):
            acc = acc - lower[j, i] * back[j]
        back[i] = acc / lower[i, i]
    return jnp.stack(back)


def local(start_field, known):
    cells = float(
        start_field.shape[0]
        * lax.axis_size("px")
        * start_field.shape[1]
        * lax.axis_size("py")
        * start_field.shape[2]
    )
    field = start_field
    lap_field = laplace(field)
    for step in range(NEWTON):
        force = allen_cahn(field, lap_field)
        diffs = field[None] - known
        dist_local = jnp.sum(diffs * diffs, axis=(1, 2, 3))
        first_sum, force_sq = lax.psum((dist_local, jnp.sum(force * force)), ("px", "py"))
        beta = jnp.sqrt(force_sq + EPS)
        basis = [-force / beta]
        lap_basis = []
        jac_diag = 1.0 - 3.0 * field * field
        hess = jnp.zeros((ITERS + 1, ITERS), jnp.float32)
        for k in range(ITERS):
            lap_vec = laplace(basis[k])
            lap_basis.append(lap_vec)
            image = DIFFUSION * lap_vec + jac_diag * basis[k]
            heights_local = jnp.stack([jnp.sum(vec * image) for vec in basis])
            summed = lax.psum(heights_local, ("px", "py"))
            rest = image
            for j in range(k + 1):
                rest = rest - summed[j] * basis[j]
            height = jnp.sqrt(lax.psum(jnp.sum(rest * rest), ("px", "py")) + EPS)
            hess = hess.at[: k + 1, k].set(summed).at[k + 1, k].set(height)
            if k < ITERS - 1:
                basis.append(rest / height)
        coeffs = solve_small(hess, beta)
        delta = coeffs[0] * basis[0]
        for j in range(1, ITERS):
            delta = delta + coeffs[j] * basis[j]
        inner = lax.psum(jnp.sum(diffs * delta[None], axis=(1, 2, 3)), ("px", "py"))
        mean_dist = first_sum / cells + EPS
        weight = 1.0 / mean_dist + SHIFT
        total = jnp.sum(2.0 * inner / (cells * mean_dist * mean_dist * weight))
        scale = 1.0 / (1.0 + jnp.abs(total))
        field = field + scale * delta
        lap_field = laplace(field)
    return (field, allen_cahn(field, lap_field))


def solution(mesh):
    placed = (P("px", "py", None), P(None, "px", "py", None))
    return jax.shard_map(
        local,
        mesh=mesh,
        in_specs=placed,
        out_specs=(P("px", "py", None), P("px", "py", None)),
        check_vma=False,
    )
```

profile of v0, /device:TPU:38, one launch (start us, length us, event | category | flops | bytes accessed | tf_op | source)
XLA Modules:
  0.0 1435.6 jit_solution(6165251050151356504)
XLA Ops:
  1.5 2.7 collective-permute-start
  4.2 5.2 collective-permute-start.1
  14.0 2.4 collective-permute-start.3
  19.9 80.0 %psum.126 = f32[]{:T(128)} all-reduce(f32[]{:T(128)} %get-tuple-element.179), channel_id=1, replica_groups=mesh['px'=16,'py'=16] {'px','py'}, use_global_device_ids=true, to_apply=%region_1.0 | all-reduce | flops 1 | bytes 8 | tf_op jit(solution)/shard_map/psum | solution.py:78
  100.6 3.4 collective-permute-start.5
  104.0 2.5 collective-permute-start.4
  107.2 4.7 collective-permute-done.4
  113.9 2.4 collective-permute-start.7
  116.5 2.5 collective-permute-done.7
  119.8 73.3 %psum.127 = f32[1]{0:T(128)} all-reduce(f32[1]{0:T(128)} %bitcast), channel_id=1, replica_groups=mesh['px'=16,'py'=16] {'px','py'}, use_global_device_ids=true, to_apply=%region_3.0 | all-reduce | flops 1 | bytes 8 | tf_op jit(solution)/shard_map/psum | solution.py:89
  194.5 74.3 %psum.128 = f32[]{:T(128)} all-reduce(f32[]{:T(128)} %multiply_reduce_fusion.21), channel_id=1, replica_groups=mesh['px'=16,'py'=16] {'px','py'}, use_global_device_ids=true, to_apply=%region_5.0 | all-reduce | flops 1 | bytes 8 | tf_op jit(solution)/shard_map/psum | solution.py:93
  270.2 3.4 collective-permute-start.9
  273.6 2.5 collective-permute-start.8
  277.3 4.1 collective-permute-done.8
  283.4 2.4 collective-permute-start.11
  291.0 73.4 %psum.129 = f32[2]{0:T(128)S(1)} all-reduce(f32[2]{0:T(128)S(1)} %pad_maximum_fusion.92), channel_id=1, replica_groups=mesh['px'=16,'py'=16] {'px','py'}, use_global_device_ids=true, to_apply=%region_9.0 | all-reduce | flops 2 | bytes 16 | tf_op jit(solution)/shard_map/psum | solution.py:89
  365.0 2.0 multiply_reduce_fusion.18
  367.1 74.1 %psum.130 = f32[]{:T(128)} all-reduce(f32[]{:T(128)} %get-tuple-element.174), channel_id=1, replica_groups=mesh['px'=16,'py'=16] {'px','py'}, use_global_device_ids=true, to_apply=%region_11.0 | all-reduce | flops 1 | bytes 8 | tf_op jit(solution)/shard_map/psum | solution.py:93
  441.9 3.4 collective-permute-start.13
  445.3 2.5 collective-permute-start.12
  448.6 4.6 collective-permute-done.12
  455.1 2.4 collective-permute-start.15
  457.5 2.0 broadcast_select_fusion.3
  461.1 2.8 multiply_reduce_fusion.17
  466.0 75.2 %psum.131 = f32[3]{0:T(128)S(1)} all-reduce(f32[3]{0:T(128)S(1)} %pad_maximum_fusion.93), channel_id=1, replica_groups=mesh['px'=16,'py'=16] {'px','py'}, use_global_device_ids=true, to_apply=%region_16.0 | all-reduce | flops 3 | bytes 24 | tf_op jit(solution)/shard_map/psum | solution.py:89
  543.7 3.6 multiply_reduce_fusion.14
  548.8 74.0 %psum.132 = f32[]{:T(128)} all-reduce(f32[]{:T(128)} %multiply_reduce_fusion.14), channel_id=1, replica_groups=mesh['px'=16,'py'=16] {'px','py'}, use_global_device_ids=true, to_apply=%region_18.0 | all-reduce | flops 1 | bytes 8 | tf_op jit(solution)/shard_map/psum | solution.py:93
  636.7 73.7 %all-reduce.21 = (f32[8]{0:T(128)S(1)}, f32[8]{0:T(128)S(1)}) all-reduce(f32[8]{0:T(128)S(1)} %get-tuple-element.150, f32[8]{0:T(128)S(1)} %get-tuple-element.149), channel_id=1, replica_groups=mesh['px'=16,'py'=16] {'px','py'}, use_global_device_ids=true, to_apply=%region_25.27 | all-reduce | flops 16 | bytes 128 | tf_op jit(solution)/shard_map/psum | solution.py:78
  711.9 3.3 collective-permute-start.17
  715.2 2.5 collective-permute-start.16
  717.7 5.4 collective-permute-done.16
  725.0 2.4 collective-permute-start.19
  727.6 2.5 collective-permute-done.19
  731.0 73.4 %psum.135 = f32[]{:T(128)} all-reduce(f32[]{:T(128)} %get-tuple-element.171), channel_id=1, replica_groups=mesh['px'=16,'py'=16] {'px','py'}, use_global_device_ids=true, to_apply=%region_28.0 | all-reduce | flops 1 | bytes 8 | tf_op jit(solution)/shard_map/psum | solution.py:78
  805.1 3.4 collective-permute-start.21
  808.5 2.5 collective-permute-start.20
  811.0 5.4 collective-permute-done.20
  818.3 2.4 collective-permute-start.23
  820.9 2.5 collective-permute-done.23
  824.3 73.4 %psum.136 = f32[1]{0:T(128)} all-reduce(f32[1]{0:T(128)} %bitcast.32), channel_id=1, replica_groups=mesh['px'=16,'py'=16] {'px','py'}, use_global_device_ids=true, to_apply=%region_30.0 | all-reduce | flops 1 | bytes 8 | tf_op jit(solution)/shard_map/psum | solution.py:89
  899.0 74.1 %psum.137 = f32[]{:T(128)} all-reduce(f32[]{:T(128)} %multiply_reduce_fusion.11), channel_id=1, replica_groups=mesh['px'=16,'py'=16] {'px','py'}, use_global_device_ids=true, to_apply=%region_32.0 | all-reduce | flops 1 | bytes 8 | tf_op jit(solution)/shard_map/psum | solution.py:93
  974.5 3.4 collective-permute-start.25
  977.9 2.5 collective-permute-start.24
  980.4 5.4 collective-permute-done.24
  987.8 2.4 collective-permute-start.27
  995.3 73.4 %psum.138 = f32[2]{0:T(128)S(1)} all-reduce(f32[2]{0:T(128)S(1)} %pad_maximum_fusion.94), channel_id=1, replica_groups=mesh['px'=16,'py'=16] {'px','py'}, use_global_device_ids=true, to_apply=%region_35.0 | all-reduce | flops 2 | bytes 16 | tf_op jit(solution)/shard_map/psum | solution.py:89
  1069.3 2.0 multiply_reduce_fusion.8
  1071.4 74.0 %psum.139 = f32[]{:T(128)} all-reduce(f32[]{:T(128)} %get-tuple-element.166), channel_id=1, replica_groups=mesh['px'=16,'py'=16] {'px','py'}, use_global_device_ids=true, to_apply=%region_37.0 | all-reduce | flops 1 | bytes 8 | tf_op jit(solution)/shard_map/psum | solution.py:93
  1146.1 3.4 collective-permute-start.29
  1149.5 2.5 collective-permute-start.28
  1152.9 4.6 collective-permute-done.28
  1160.0 2.4 collective-permute-start.31
  1162.4 2.0 broadcast_select_fusion.2
  1166.0 2.7 multiply_reduce_fusion.7
  1168.6 2.0 pad_maximum_fusion.95
  1170.8 75.2 %psum.140 = f32[3]{0:T(128)S(1)} all-reduce(f32[3]{0:T(128)S(1)} %pad_maximum_fusion.95), channel_id=1, replica_groups=mesh['px'=16,'py'=16] {'px','py'}, use_global_device_ids=true, to_apply=%region_41.0 | all-reduce | flops 3 | bytes 24 | tf_op jit(solution)/shard_map/psum | solution.py:89
  1248.5 3.6 multiply_reduce_fusion.4
  1253.5 74.1 %psum.141 = f32[]{:T(128)} all-reduce(f32[]{:T(128)} %multiply_reduce_fusion.4), channel_id=1, replica_groups=mesh['px'=16,'py'=16] {'px','py'}, use_global_device_ids=true, to_apply=%region_43.0 | all-reduce | flops 1 | bytes 8 | tf_op jit(solution)/shard_map/psum | solution.py:93
  1341.6 73.5 %all-reduce.20 = (f32[8]{0:T(128)S(1)}, f32[8]{0:T(128)S(1)}) all-reduce(f32[8]{0:T(128)S(1)} %get-tuple-element.148, f32[8]{0:T(128)S(1)} %get-tuple-element.147), channel_id=1, replica_groups=mesh['px'=16,'py'=16] {'px','py'}, use_global_device_ids=true, to_apply=%region_48.0 | all-reduce | flops 16 | bytes 128 | tf_op jit(solution)/shard_map/psum | solution.py:78
  1416.4 3.3 collective-permute-start.33
  1419.8 2.5 collective-permute-start.32
  1422.3 5.4 collective-permute-done.32
  1429.6 2.4 collective-permute-start.35
  1432.2 2.5 collective-permute-done.35
  (141 shorter events, 70.3 us)
Async XLA Ops:
  0.6 18.4 %copy-start = (f32[8,16,512]{2,1,0:T(8,128)S(1)}, f32[8,16,512]{2,1,0:T(8,128)}, u32[]{:S(2)}) copy-start(f32[8,16,512]{2,1,0:T(8,128)} %param.27) | copy-start | bytes 786436
  1.5 10.5 collective-permute-start
  4.2 6.8 collective-permute-start.1
  12.0 5.6 collective-permute-start.2
  14.0 5.1 collective-permute-start.3
  100.6 6.5 collective-permute-start.5
  104.0 7.9 collective-permute-start.4
  112.0 4.5 collective-permute-start.6
  113.9 5.1 collective-permute-start.7
  270.2 7.1 collective-permute-start.9
  273.6 7.9 collective-permute-start.8
  281.5 5.1 collective-permute-start.10
  283.4 5.1 collective-permute-start.11
  441.9 6.7 collective-permute-start.13
  445.3 7.9 collective-permute-start.12
  453.2 7.9 collective-permute-start.14
  455.1 6.0 collective-permute-start.15
  461.1 175.0 %copy-start.1 = (f32[8,8,16,512]{3,2,1,0:T(8,128)S(1)}, f32[8,8,16,512]{3,2,1,0:T(8,128)}, u32[]{:S(2)}) copy-start(f32[8,8,16,512]{3,2,1,0:T(8,128)} %param.28) | copy-start | bytes 6291460
  711.9 5.9 collective-permute-start.17
  715.2 7.9 collective-permute-start.16
  723.1 4.5 collective-permute-start.18
  725.0 5.1 collective-permute-start.19
  805.1 5.9 collective-permute-start.21
  808.5 7.9 collective-permute-start.20
  816.4 4.5 collective-permute-start.22
  818.3 5.1 collective-permute-start.23
  974.5 5.9 collective-permute-start.25
  977.9 7.9 collective-permute-start.24
  985.8 5.1 collective-permute-start.26
  987.8 5.1 collective-permute-start.27
  1146.1 6.7 collective-permute-start.29
  1149.5 7.9 collective-permute-start.28
  1158.1 7.9 collective-permute-start.30
  1160.0 6.0 collective-permute-start.31
  1416.4 19.2 %copy-start.2 = (f32[8,16,512]{2,1,0:T(8,128)}, f32[8,16,512]{2,1,0:T(8,128)S(1)}, u32[]{:S(2)}) copy-start(f32[8,16,512]{2,1,0:T(8,128)S(1)} %multiply_add_fusion) | copy-start | bytes 786436
  1416.4 5.9 collective-permute-start.33
  1419.8 7.9 collective-permute-start.32
  1427.7 4.5 collective-permute-start.34
  1429.6 5.1 collective-permute-start.35
where the time goes:
time: 1440 us
  blocking collectives  1190 us (83%)
  starting transfers between devices  93.6 us (6%)
  waiting for transfers between devices  55.3 us (4%)
  other arithmetic  50.1 us (3%)
  between operations  27.2 us (2%)
  local copies, waits for them, and re-layouts  20.1 us (1%)
    psum x6, blocking collectives, local(): height = jnp.sqrt(lax.psum(jnp.sum(rest * rest), ('px', 'py')) + EPS)  445 us
    psum x6, blocking collectives, local(): summed = lax.psum(heights_local, ('px', 'py'))  444 us
    psum x4, blocking collectives, local(): lax.psum((dist_local, jnp.sum(force * force)), ('px', 'py'))  301 us
    ppermute x18, starting transfers between devices, extended(): lax.ppermute(tail, axis, [(i, (i + 1) % count) for i in range(ends)])  53.6 us
    ppermute x18, starting transfers between devices, extended(): lax.ppermute(head, axis, [((i + 1) % count, i) for i in range(ends)])  40 us
    ppermute x18, waiting for transfers between devices, extended(): lax.ppermute(head, axis, [((i + 1) % count, i) for i in range(ends)])  39.6 us
  transfers between devices with their start and end apart: 36, of which 16 were waited for; matrix products, arithmetic and copies ran while one was open for 1% of the time, Pallas kernels for 0%

commit v1 on v0

--- a/solution.py
+++ b/solution.py
@@ -86,7 +86,8 @@
             lap_basis.append(lap_vec)
             image = DIFFUSION * lap_vec + jac_diag * basis[k]
             heights_local = jnp.stack([jnp.sum(vec * image) for vec in basis])
-            summed = lax.psum(heights_local, ("px", "py"))
+            parts = lax.all_gather(heights_local, ("px", "py"), axis=0, tiled=False)
+            summed = parts.sum(axis=0)
             rest = image
             for j in range(k + 1):
                 rest = rest - summed[j] * basis[j]

time: 1440 us -> 1440 us (level)
  waiting for transfers between devices: 55.3 us -> 26.5 us
  starting transfers between devices: 93.6 us -> 108 us
    unnamed x0 -> x6, blocking collectives: none -> 453 us
    psum x6 -> x0, blocking collectives: 444 us -> none  [local(): summed = lax.psum(heights_local, ('px', 'py'))]
    ppermute x18, waiting for transfers between devices: 39.6 us -> 3.31 us  [extended(): lax.ppermute(head, axis, [((i + 1) % count, i) for i in range(ends)])]
    ppermute x18, starting transfers between devices: 53.6 us -> 71.7 us  [extended(): lax.ppermute(tail, axis, [(i, (i + 1) % count) for i in range(ends)])]
where the time goes in v1:
time: 1440 us
  blocking collectives  1200 us (83%)
  starting transfers between devices  108 us (8%)
  other arithmetic  53.1 us (4%)
  between operations  27.5 us (2%)
  waiting for transfers between devices  26.5 us (2%)
  local copies, waits for them, and re-layouts  22.8 us (2%)
    unnamed x6, blocking collectives  453 us
    psum x6, blocking collectives, local(): height = jnp.sqrt(lax.psum(jnp.sum(rest * rest), ('px', 'py')) + EPS)  446 us
    psum x4, blocking collectives, local(): lax.psum((dist_local, jnp.sum(force * force)), ('px', 'py'))  299 us
    ppermute x18, starting transfers between devices, extended(): lax.ppermute(tail, axis, [(i, (i + 1) % count) for i in range(ends)])  71.7 us
    ppermute x18, starting transfers between devices, extended(): lax.ppermute(head, axis, [((i + 1) % count, i) for i in range(ends)])  36.7 us
  transfers between devices with their start and end apart: 36, of which 16 were waited for; matrix products, arithmetic and copies ran while one was open for 1% of the time, Pallas kernels for 0%

profile of v1, /device:TPU:38, one launch (start us, length us, event | category | flops | bytes accessed | tf_op | source)
XLA Modules:
  0.0 1436.0 jit_solution(16213385688685286768)
XLA Ops:
  1.5 3.4 collective-permute-start.1
  4.9 2.4 collective-permute-start
  9.5 3.3 collective-permute-done
  12.8 1.9 collective-permute-start.2
  14.8 2.4 collective-permute-start.3
  20.7 76.8 %psum.84 = f32[]{:T(128)} all-reduce(f32[]{:T(128)} %get-tuple-element.179), channel_id=1, replica_groups=mesh['px'=16,'py'=16] {'px','py'}, use_global_device_ids=true, to_apply=%region_1.0 | all-reduce | flops 1 | bytes 8 | tf_op jit(solution)/shard_map/psum | solution.py:78
  98.2 2.5 collective-permute-start.4
  100.7 5.4 collective-permute-start.5
  107.8 1.9 collective-permute-start.6
  109.7 2.4 collective-permute-start.7
  112.3 2.5 collective-permute-done.7
  116.4 74.7 %all-reduce.20 = f32[256]{0:T(256)S(1)} all-reduce(f32[256]{0:T(256)S(1)} %dynamic-update-slice.26), channel_id=1, replica_groups=mesh['px'=16,'py'=16] {'px','py'}, use_global_device_ids=true, to_apply=%add.20 | all-reduce | flops 256 | bytes 2048
  193.0 74.3 %psum.85 = f32[]{:T(128)} all-reduce(f32[]{:T(128)} %multiply_reduce_fusion.21), channel_id=1, replica_groups=mesh['px'=16,'py'=16] {'px','py'}, use_global_device_ids=true, to_apply=%region_5.0 | all-reduce | flops 1 | bytes 8 | tf_op jit(solution)/shard_map/psum | solution.py:94
  268.7 1.9 collective-permute-start.8
  270.6 6.0 collective-permute-start.9
  278.2 1.9 collective-permute-start.10
  280.2 2.4 collective-permute-start.11
  287.6 74.7 %all-reduce.21 = f32[512]{0:T(512)S(1)} all-reduce(f32[512]{0:T(512)S(1)} %maximum_dynamic-update-slice_fusion), channel_id=2, replica_groups=mesh['px'=16,'py'=16] {'px','py'}, use_global_device_ids=true, to_apply=%add.21 | all-reduce | flops 512 | bytes 4096
  363.0 2.1 multiply_reduce_fusion.18
  365.1 74.5 %psum.86 = f32[]{:T(128)} all-reduce(f32[]{:T(128)} %get-tuple-element.174), channel_id=1, replica_groups=mesh['px'=16,'py'=16] {'px','py'}, use_global_device_ids=true, to_apply=%region_11.0 | all-reduce | flops 1 | bytes 8 | tf_op jit(solution)/shard_map/psum | solution.py:94
  440.4 1.9 collective-permute-start.12
  442.3 6.0 collective-permute-start.13
  450.0 1.9 collective-permute-start.14
  451.9 2.4 collective-permute-start.15
  454.3 2.0 broadcast_select_fusion.3
  457.9 2.8 multiply_reduce_fusion.17
  460.7 2.1 maximum_dynamic-update-slice_fusion.1
  462.8 76.4 %all-reduce.22 = f32[768]{0:T(1024)S(1)} all-reduce(f32[768]{0:T(1024)S(1)} %maximum_dynamic-update-slice_fusion.1), channel_id=3, replica_groups=mesh['px'=16,'py'=16] {'px','py'}, use_global_device_ids=true, to_apply=%add.22 | all-reduce | flops 768 | bytes 6144
  540.0 3.6 multiply_reduce_fusion.14
  543.7 74.4 %psum.87 = f32[]{:T(128)} all-reduce(f32[]{:T(128)} %multiply_reduce_fusion.14), channel_id=1, replica_groups=mesh['px'=16,'py'=16] {'px','py'}, use_global_device_ids=true, to_apply=%region_18.0 | all-reduce | flops 1 | bytes 8 | tf_op jit(solution)/shard_map/psum | solution.py:94
  635.6 73.4 %all-reduce.27 = (f32[8]{0:T(128)S(1)}, f32[8]{0:T(128)S(1)}) all-reduce(f32[8]{0:T(128)S(1)} %get-tuple-element.150, f32[8]{0:T(128)S(1)} %get-tuple-element.149), channel_id=1, replica_groups=mesh['px'=16,'py'=16] {'px','py'}, use_global_device_ids=true, to_apply=%region_25.27 | all-reduce | flops 16 | bytes 128 | tf_op jit(solution)/shard_map/psum | solution.py:78
  710.4 1.9 collective-permute-start.16
  712.3 6.0 collective-permute-start.17
  719.9 1.9 collective-permute-start.18
  721.9 2.4 collective-permute-start.19
  724.4 2.5 collective-permute-done.19
  727.8 74.5 %psum.90 = f32[]{:T(128)} all-reduce(f32[]{:T(128)} %get-tuple-element.171), channel_id=1, replica_groups=mesh['px'=16,'py'=16] {'px','py'}, use_global_device_ids=true, to_apply=%region_28.0 | all-reduce | flops 1 | bytes 8 | tf_op jit(solution)/shard_map/psum | solution.py:78
  803.0 3.0 collective-permute-start.20
  805.9 5.0 collective-permute-start.21
  812.6 1.9 collective-permute-start.22
  814.5 2.4 collective-permute-start.23
  817.1 2.5 collective-permute-done.23
  821.2 75.8 %all-reduce.23 = f32[256]{0:T(256)S(1)} all-reduce(f32[256]{0:T(256)S(1)} %dynamic-update-slice.29), channel_id=1, replica_groups=mesh['px'=16,'py'=16] {'px','py'}, use_global_device_ids=true, to_apply=%add.23 | all-reduce | flops 256 | bytes 2048
  898.9 74.2 %psum.91 = f32[]{:T(128)} all-reduce(f32[]{:T(128)} %multiply_reduce_fusion.11), channel_id=1, replica_groups=mesh['px'=16,'py'=16] {'px','py'}, use_global_device_ids=true, to_apply=%region_32.0 | all-reduce | flops 1 | bytes 8 | tf_op jit(solution)/shard_map/psum | solution.py:94
  974.6 1.9 collective-permute-start.24
  976.5 6.0 collective-permute-start.25
  984.1 1.9 collective-permute-start.26
  986.1 2.4 collective-permute-start.27
  994.6 75.3 %all-reduce.24 = f32[512]{0:T(512)S(1)} all-reduce(f32[512]{0:T(512)S(1)} %maximum_dynamic-update-slice_fusion.2), channel_id=4, replica_groups=mesh['px'=16,'py'=16] {'px','py'}, use_global_device_ids=true, to_apply=%add.24 | all-reduce | flops 512 | bytes 4096
  1070.6 2.0 multiply_reduce_fusion.8
  1072.7 74.5 %psum.92 = f32[]{:T(128)} all-reduce(f32[]{:T(128)} %get-tuple-element.166), channel_id=1, replica_groups=mesh['px'=16,'py'=16] {'px','py'}, use_global_device_ids=true, to_apply=%region_37.0 | all-reduce | flops 1 | bytes 8 | tf_op jit(solution)/shard_map/psum | solution.py:94
  1147.9 1.9 collective-permute-start.28
  1149.8 6.0 collective-permute-start.29
  1160.0 2.4 collective-permute-start.31
  1162.4 2.0 broadcast_select_fusion.2
  1166.0 2.7 multiply_reduce_fusion.7
  1168.7 2.1 maximum_dynamic-update-slice_fusion.3
  1170.8 76.4 %all-reduce.25 = f32[768]{0:T(1024)S(1)} all-reduce(f32[768]{0:T(1024)S(1)} %maximum_dynamic-update-slice_fusion.3), channel_id=5, replica_groups=mesh['px'=16,'py'=16] {'px','py'}, use_global_device_ids=true, to_apply=%add.25 | all-reduce | flops 768 | bytes 6144
  1248.1 3.7 multiply_reduce_fusion.4
  1251.9 73.7 %psum.93 = f32[]{:T(128)} all-reduce(f32[]{:T(128)} %multiply_reduce_fusion.4), channel_id=1, replica_groups=mesh['px'=16,'py'=16] {'px','py'}, use_global_device_ids=true, to_apply=%region_43.0 | all-reduce | flops 1 | bytes 8 | tf_op jit(solution)/shard_map/psum | solution.py:94
  1342.9 74.2 %all-reduce.26 = (f32[8]{0:T(128)S(1)}, f32[8]{0:T(128)S(1)}) all-reduce(f32[8]{0:T(128)S(1)} %get-tuple-element.148, f32[8]{0:T(128)S(1)} %get-tuple-element.147), channel_id=1, replica_groups=mesh['px'=16,'py'=16] {'px','py'}, use_global_device_ids=true, to_apply=%region_48.0 | all-reduce | flops 16 | bytes 128 | tf_op jit(solution)/shard_map/psum | solution.py:78
  1420.4 6.0 collective-permute-start.33
  1430.0 2.4 collective-permute-start.35
  1432.5 2.5 collective-permute-done.35
  (159 shorter events, 69.7 us)
Async XLA Ops:
  0.6 19.2 %copy-start = (f32[8,16,512]{2,1,0:T(8,128)S(1)}, f32[8,16,512]{2,1,0:T(8,128)}, u32[]{:S(2)}) copy-start(f32[8,16,512]{2,1,0:T(8,128)} %param.27) | copy-start | bytes 786436
  1.5 7.1 collective-permute-start.1
  4.9 7.9 collective-permute-start
  12.8 5.7 collective-permute-start.2
  14.8 5.1 collective-permute-start.3
  98.2 8.6 collective-permute-start.4
  100.7 7.0 collective-permute-start.5
  107.8 4.5 collective-permute-start.6
  109.7 5.1 collective-permute-start.7
  268.7 9.2 collective-permute-start.8
  270.6 7.6 collective-permute-start.9
  278.2 5.3 collective-permute-start.10
  280.2 5.1 collective-permute-start.11
  440.4 8.8 collective-permute-start.12
  442.3 7.6 collective-permute-start.13
  450.0 7.9 collective-permute-start.14
  451.9 6.0 collective-permute-start.15
  457.9 177.2 %copy-start.1 = (f32[8,8,16,512]{3,2,1,0:T(8,128)S(1)}, f32[8,8,16,512]{3,2,1,0:T(8,128)}, u32[]{:S(2)}) copy-start(f32[8,8,16,512]{3,2,1,0:T(8,128)} %param.28) | copy-start | bytes 6291460
  710.4 8.0 collective-permute-start.16
  712.3 7.6 collective-permute-start.17
  719.9 4.5 collective-permute-start.18
  721.9 5.1 collective-permute-start.19
  803.0 8.0 collective-permute-start.20
  805.9 6.6 collective-permute-start.21
  812.6 4.5 collective-permute-start.22
  814.5 5.1 collective-permute-start.23
  974.6 8.0 collective-permute-start.24
  976.5 7.6 collective-permute-start.25
  984.1 5.9 collective-permute-start.26
  986.1 5.1 collective-permute-start.27
  1147.9 8.8 collective-permute-start.28
  1149.8 7.6 collective-permute-start.29
  1158.1 7.9 collective-permute-start.30
  1160.0 6.0 collective-permute-start.31
  1418.4 17.5 %copy-start.2 = (f32[8,16,512]{2,1,0:T(8,128)}, f32[8,16,512]{2,1,0:T(8,128)S(1)}, u32[]{:S(2)}) copy-start(f32[8,16,512]{2,1,0:T(8,128)S(1)} %multiply_add_fusion) | copy-start | bytes 786436
  1418.5 8.0 collective-permute-start.32
  1420.4 7.6 collective-permute-start.33
  1428.0 4.5 collective-permute-start.34
  1430.0 5.1 collective-permute-start.35
